TPU v7x, 32 devices: a whole 2x2x4 slice. The times are simulated.
32 devices in a mesh: fsdp: 8 (over z, core), seq: 4 (over y, x).
Axes of the slice: x: 2, y: 2, z: 4, core: 2. Of those that a mesh axis runs over, the one named last changes fastest.
Arguments:
- inputs: bfloat16 [8, 1024, 2048], P('fsdp', 'seq'), may hold values from -6 to 6
- cotangent: bfloat16 [8, 1024, 2048], P('fsdp', 'seq'), may hold values from -6 to 6
- norm1_gain: bfloat16 [2048], P('fsdp'), may hold values from 0.5 to 1.5
- w_qkv: bfloat16 [2048, 6144], P('fsdp'), may hold values from -0.125 to 0.125
- w_beta: bfloat16 [2048, 16], P('fsdp'), may hold values from -0.125 to 0.125
- conv_weight: bfloat16 [2048, 12], P('fsdp'), may hold values from -3 to 3
- out_gain: bfloat16 [128], replicated, may hold values from 0.5 to 1.5
- w_out: bfloat16 [2048, 2048], P('fsdp'), may hold values from -0.125 to 0.125
- norm2_gain: bfloat16 [2048], P('fsdp'), may hold values from 0.5 to 1.5
- w_gate_up: bfloat16 [2048, 11264], P('fsdp'), may hold values from -0.125 to 0.125
- w_down: bfloat16 [5632, 2048], P('fsdp'), may hold values from -0.15625 to 0.15625
Outputs:
- output: bfloat16 [8, 1024, 2048], P('fsdp', 'seq')
- grad_input: float32 [8, 1024, 2048], P('fsdp', 'seq')
- grad_norm1_gain: float32 [2048], P('fsdp')
- grad_w_qkv: float32 [2048, 6144], P('fsdp')
- grad_w_beta: float32 [2048, 16], P('fsdp')
- grad_conv_weight: float32 [2048, 12], P('fsdp')
- grad_out_gain: float32 [128], replicated
- grad_w_out: float32 [2048, 2048], P('fsdp')
- grad_norm2_gain: float32 [2048], P('fsdp')
- grad_w_gate_up: float32 [2048, 11264], P('fsdp')
- grad_w_down: float32 [5632, 2048], P('fsdp')
All inputs are finite; a program needn't handle non-finite values.
Results may differ from a plain program's by a relative error of at most 0.023.
Values may be sent and summed in bfloat16 or wider, within the bound.
A program may use at most 448 MiB of HBM per device.

v0:
```python
import jax
import jax.numpy as jnp
from jax import lax
from jax.sharding import PartitionSpec as P

H = 16
DK = 128
SPAN = 64
EPS = 1e-06
HIGH = lax.Precision.HIGHEST


def from_behind(array, axis, by):
    devices = lax.axis_size(axis)
    pairs = [(i, i + by) for i in range(devices) if 0 <= i + by < devices]
    return lax.ppermute(array, axis, pairs)


def rms_scale(values, gain):
    return values * lax.rsqrt(jnp.mean(values * values, axis=-1, keepdims=True) + EPS) * gain


def conv_table(conv_full):
    width = conv_full.shape[0]
    tap_count = conv_full.shape[1] // 3
    return (
        conv_full.astype(jnp.float32)
        .reshape(width, 3, tap_count)
        .transpose(1, 0, 2)
        .reshape(3 * width, tap_count)
    )


def pre_mix(extended, table, beta_logits):
    tap_count = table.shape[1]
    length = extended.shape[1] - tap_count + 1
    sequences = extended.shape[0]
    width = extended.shape[2] // 3
    mixed = extended[:, 0:length, :] * table[:, 0]
    for tap_index in range(1, tap_count):
        mixed = mixed + extended[:, tap_index : tap_index + length, :] * table[:, tap_index]
    active = jax.nn.silu(mixed)
    query = active[:, :, :width].reshape(sequences, length, H, DK) * DK ** (-0.5)
    key = active[:, :, width : 2 * width].reshape(sequences, length, H, DK)
    key = key * lax.rsqrt(jnp.sum(key * key, axis=-1, keepdims=True) + EPS)
    value = active[:, :, 2 * width :].reshape(sequences, length, H, DK)
    return (query, key, value, jax.nn.sigmoid(beta_logits))


def delta_rule(query, key, value, beta):
    sequences, length, heads, depth = query.shape
    count = length // SPAN

    def blocks(array):
        return array.reshape(sequences, count, SPAN, heads, -1).transpose(1, 0, 3, 2, 4)

    q_blocks = blocks(query)
    k_blocks = blocks(key)
    v_blocks = blocks(value)
    b_blocks = blocks(beta[..., None])
    gram = jnp.einsum("nshcd,nshmd->nshcm", k_blocks, k_blocks, precision=HIGH)
    below = jnp.tril(jnp.ones((SPAN, SPAN), jnp.float32), -1)
    inclusive = jnp.tril(jnp.ones((SPAN, SPAN), jnp.float32))
    system = jnp.eye(SPAN, dtype=jnp.float32) + below * (b_blocks * gram)
    targets = jnp.concatenate([b_blocks * k_blocks, b_blocks * v_blocks], axis=-1)
    solved = lax.linalg.triangular_solve(
        system, targets, left_side=True, lower=True, unit_diagonal=True
    )
    wy_key = solved[..., :depth]
    wy_value = solved[..., depth:]
    within = inclusive * jnp.einsum("nshcd,nshmd->nshcm", q_blocks, k_blocks, precision=HIGH)

    def advance(state, pieces):
        key_part, value_part, query_part, key_raw, attend = pieces
        fresh = value_part - jnp.einsum("shcd,shde->shce", key_part, state, precision=HIGH)
        result = jnp.einsum("shcd,shde->shce", query_part, state, precision=HIGH)
        result = result + jnp.einsum("shcm,shme->shce", attend, fresh, precision=HIGH)
        state = state + jnp.einsum("shcd,shce->shde", key_raw, fresh, precision=HIGH)
        return (state, result)

    start = jnp.zeros((sequences, heads, depth, value.shape[-1]), jnp.float32)
    final, outputs = lax.scan(advance, start, (wy_key, wy_value, q_blocks, k_blocks, within))
    return outputs.transpose(1, 0, 3, 2, 4).reshape(sequences, length, heads, -1)


def row_term(left, right):

    def term(start, count):
        return lax.dot_general(
            left, right, (((0,), (0,)), ((), ())), preferred_element_type=jnp.float32
        )

    return term


def reduce_rows(term, total_rows):
    shards = lax.axis_size("fsdp")
    summed = lax.psum_scatter(
        term(jnp.int32(0), total_rows // shards * lax.axis_size("fsdp")).astype(jnp.bfloat16),
        "fsdp",
        scatter_dimension=0,
        tiled=True,
    )
    return lax.psum(summed, "seq").astype(jnp.float32)


def against(left, right):
    return lax.dot_general(
        left, right, (((1,), (1,)), ((), ())), preferred_element_type=jnp.float32
    )


def per_device(
    inputs,
    cotangent,
    norm1_gain,
    w_qkv,
    w_beta,
    conv_weight,
    out_gain,
    w_out,
    norm2_gain,
    w_gate_up,
    w_down,
):
    gathered = (
        lax.all_gather(norm1_gain, "fsdp", axis=0, tiled=True),
        lax.all_gather(w_qkv, "fsdp", axis=0, tiled=True),
        lax.all_gather(w_beta, "fsdp", axis=0, tiled=True),
        lax.all_gather(conv_weight, "fsdp", axis=0, tiled=True),
        lax.all_gather(w_out, "fsdp", axis=0, tiled=True),
        lax.all_gather(norm2_gain, "fsdp", axis=0, tiled=True),
        lax.all_gather(w_gate_up, "fsdp", axis=0, tiled=True),
    )
    gain_first, qkv_full, beta_full, conv_full, out_full, gain_second, gate_up_full = gathered
    down_full = lax.all_gather(w_down, "fsdp", axis=0, tiled=True)
    sequences, block, width = inputs.shape
    tokens = sequences * block
    hidden_width = down_full.shape[0]
    edge_rows = conv_full.shape[1] // 3 - 1
    residual = inputs.astype(jnp.float32).reshape(tokens, width)
    first_normed, first_back = jax.vjp(rms_scale, residual, gain_first.astype(jnp.float32))
    normed_first = first_normed.astype(jnp.bfloat16)
    projected = jnp.dot(normed_first, qkv_full, preferred_element_type=jnp.float32)
    projected = projected.astype(jnp.bfloat16).reshape(sequences, block, 3 * width)
    beta_logits = jnp.dot(normed_first, beta_full, preferred_element_type=jnp.float32).reshape(
        sequences, block, -1
    )
    before = from_behind(projected[:, block - edge_rows :, :], "seq", 1)
    extended = jnp.concatenate([before, projected], axis=1).astype(jnp.float32)
    table = conv_table(conv_full)
    mixer_inputs, mixer_back = jax.vjp(pre_mix, extended, table, beta_logits)
    sent_query = mixer_inputs[0].astype(jnp.bfloat16)
    sent_key = mixer_inputs[1].astype(jnp.bfloat16)
    sent_value = mixer_inputs[2].astype(jnp.bfloat16)
    sent_beta = mixer_inputs[3].astype(jnp.bfloat16)
    query, key, value, beta = (
        lax.all_to_all(sent_query, "seq", split_axis=2, concat_axis=1, tiled=True),
        lax.all_to_all(sent_key, "seq", split_axis=2, concat_axis=1, tiled=True),
        lax.all_to_all(sent_value, "seq", split_axis=2, concat_axis=1, tiled=True),
        lax.all_to_all(sent_beta, "seq", split_axis=2, concat_axis=1, tiled=True),
    )
    heads_out, delta_back = jax.vjp(
        delta_rule,
        query.astype(jnp.float32),
        key.astype(jnp.float32),
        value.astype(jnp.float32),
        beta.astype(jnp.float32),
    )
    returned = lax.all_to_all(
        heads_out.astype(jnp.bfloat16), "seq", split_axis=1, concat_axis=2, tiled=True
    )
    normed_heads, heads_back = jax.vjp(
        rms_scale, returned.astype(jnp.float32), out_gain.astype(jnp.float32)
    )
    attn_in = normed_heads.astype(jnp.bfloat16).reshape(tokens, width)
    middle = residual + jnp.dot(attn_in, out_full, preferred_element_type=jnp.float32)
    second_normed, second_back = jax.vjp(rms_scale, middle, gain_second.astype(jnp.float32))
    ffn_in = second_normed.astype(jnp.bfloat16)
    gate_up = jnp.dot(ffn_in, gate_up_full, preferred_element_type=jnp.float32)
    gate = gate_up[:, :hidden_width]
    upward = gate_up[:, hidden_width:]
    sigma = jax.nn.sigmoid(gate)
    hidden = (gate * sigma * upward).astype(jnp.bfloat16)
    result = middle + jnp.dot(hidden, down_full, preferred_element_type=jnp.float32)
    output = result.astype(jnp.bfloat16).reshape(sequences, block, width)
    upstream = cotangent.reshape(tokens, width)
    grad_down = reduce_rows(row_term(hidden, upstream), hidden_width)
    grad_hidden = against(upstream, down_full)
    grad_gate = grad_hidden * upward * sigma * (1.0 + gate * (1.0 - sigma))
    grad_up = grad_hidden * gate * sigma
    grad_gate_up = jnp.concatenate([grad_gate, grad_up], axis=1).astype(jnp.bfloat16)
    grad_w_gate_up = reduce_rows(row_term(ffn_in, grad_gate_up), width)
    grad_ffn_in = against(grad_gate_up, gate_up_full)
    grad_middle_norm, grad_gain_second = second_back(grad_ffn_in)
    grad_middle = upstream.astype(jnp.float32) + grad_middle_norm
    grad_branch = grad_middle.astype(jnp.bfloat16)
    grad_w_out = reduce_rows(row_term(attn_in, grad_branch), width)
    grad_attn_in = against(grad_branch, out_full).reshape(sequences, block, H, DK)
    grad_returned, grad_gain_heads = heads_back(grad_attn_in)
    grad_heads = lax.all_to_all(
        grad_returned.astype(jnp.bfloat16), "seq", split_axis=2, concat_axis=1, tiled=True
    )
    grad_query, grad_key, grad_value, grad_beta = delta_back(grad_heads.astype(jnp.float32))
    back_query, back_key, back_value, back_beta = (
        lax.all_to_all(
            grad_query.astype(jnp.bfloat16), "seq", split_axis=1, concat_axis=2, tiled=True
        ),
        lax.all_to_all(
            grad_key.astype(jnp.bfloat16), "seq", split_axis=1, concat_axis=2, tiled=True
        ),
        lax.all_to_all(
            grad_value.astype(jnp.bfloat16), "seq", split_axis=1, concat_axis=2, tiled=True
        ),
        lax.all_to_all(
            grad_beta.astype(jnp.bfloat16), "seq", split_axis=1, concat_axis=2, tiled=True
        ),
    )
    grad_extended, grad_table, grad_logits = mixer_back(
        (
            back_query.astype(jnp.float32),
            back_key.astype(jnp.float32),
            back_value.astype(jnp.float32),
            back_beta.astype(jnp.float32),
        )
    )
    after = from_behind(grad_extended[:, :edge_rows, :].astype(jnp.bfloat16), "seq", -1).astype(
        jnp.float32
    )
    grad_projected = grad_extended[:, edge_rows:, :]
    grad_projected = grad_projected.at[:, block - edge_rows :, :].add(after)
    grad_proj_low = grad_projected.astype(jnp.bfloat16).reshape(tokens, 3 * width)
    grad_logits_low = grad_logits.astype(jnp.bfloat16).reshape(tokens, -1)
    grad_w_qkv = reduce_rows(row_term(normed_first, grad_proj_low), width)
    grad_beta_full = lax.dot_general(
        normed_first, grad_logits_low, (((0,), (0,)), ((), ())), preferred_element_type=jnp.float32
    )
    grad_normed_first = against(grad_proj_low, qkv_full) + against(grad_logits_low, beta_full)
    grad_residual_norm, grad_gain_first = first_back(grad_normed_first)
    grad_input = (grad_middle + grad_residual_norm).reshape(sequences, block, width)
    grad_conv = grad_table.reshape(3, width, -1).transpose(1, 0, 2).reshape(width, -1)
    summed = lax.psum(
        (grad_gain_first, grad_beta_full, grad_conv, grad_gain_heads, grad_gain_second),
        ("fsdp", "seq"),
    )
    share = width // lax.axis_size("fsdp")
    offset = lax.axis_index("fsdp") * share

    def own_rows(array):
        return lax.dynamic_slice_in_dim(array, offset, share, 0)

    return (
        output,
        grad_input,
        own_rows(summed[0]),
        grad_w_qkv,
        own_rows(summed[1]),
        own_rows(summed[2]),
        summed[3],
        grad_w_out,
        own_rows(summed[4]),
        grad_w_gate_up,
        grad_down,
    )


def solution(mesh):
    in_specs = (
        P("fsdp", "seq", None),
        P("fsdp", "seq", None),
        P("fsdp"),
        P("fsdp", None),
        P("fsdp", None),
        P("fsdp", None),
        P(),
        P("fsdp", None),
        P("fsdp"),
        P("fsdp", None),
        P("fsdp", None),
    )
    out_specs = (
        P("fsdp", "seq", None),
        P("fsdp", "seq", None),
        P("fsdp"),
        P("fsdp", None),
        P("fsdp", None),
        P("fsdp", None),
        P(),
        P("fsdp", None),
        P("fsdp"),
        P("fsdp", None),
        P("fsdp", None),
    )
    return jax.shard_map(
        per_device, mesh=mesh, in_specs=in_specs, out_specs=out_specs, check_vma=False
    )
```

profile of v0, /device:TPU:0, one launch (start us, length us, event | category | flops | bytes accessed | tf_op | source)
XLA Modules:
  0.0 2502.2 jit_solution(38190960428922679)
XLA Ops:
  10.1 13.6 all-gather
  23.7 24.1 all_gather.27
  54.7 25.3 %all_gather.26 = bf16[2048,12]{0,1:T(8,128)(2,1)S(1)} all-gather(bf16[256,12]{0,1:T(8,128)(2,1)S(1)} %copy-done.77), channel_id=1, replica_groups=mesh['fsdp'=8,'seq'=4] {'fsdp'}, dimensions={0}, use_global_device_ids=true | all-gather | bytes 55296 | tf_op jit(solution)/shard_map/all_gather | solution.py:130
  80.0 153.2 %all-gather.7.cloned.1.call-done = bf16[2048,6144]{1,0:T(8,128)(2,1)} async-done(((bf16[256,6144]{1,0:T(8,128)(2,1)}), bf16[2048,6144]{1,0:T(8,128)(2,1)}) %all-gather.7.cloned.1.call-update) | async-done | bytes 25165840 | tf_op jit(solution)/shard_map/all_gather | solution.py:128
  233.2 12.3 fusion.79
  268.5 12.8 all-to-all-done
  287.6 11.2 all-to-all-done.3
  306.9 10.2 all-to-all-done.2
  322.4 315.2 %custom-call.7 = f32[16,1,4,1,64,64]{4,5,3,2,1,0:T(8,128)S(1)} custom-call(f32[16,1,4,1,64,64]{5,4,3,2,1,0:T(8,128)} %add_bitcast_fusion), custom_call_target="InvertDiagBlocksLowerTriangular" | custom-call | tf_op jit(solution)/shard_map/jvp()/triangular_solve | solution.py:66
  653.0 107.2 %while.43 = (s32[]{:T(128)}, f32[1,4,128,128]{3,2,1,0:T(8,128)S(1)}, bf16[16,1,4,64,128]{4,3,0,2,1:T(8,128)(2,1)}, f32[16,1,4,128,128]{4,3,2,1,0:T(8,128)}, f32[...) while((s32[]{:T(128)}, ...), condition=%wide.region_3.4_spmd.clone, body=%wide.region_2.3_spmd.clone.sunk | while | flops 176553984 | bytes 3148948 | solution.py:82
  768.4 8.8 all-gather.1
  803.1 24.2 fusion.211
  827.3 83.8 %all-gather.13.cloned.1.call-done = bf16[5632,2048]{1,0:T(8,128)(2,1)} async-done(((bf16[704,2048]{1,0:T(8,128)(2,1)}), bf16[5632,2048]{1,0:T(8,128)(2,1)}) %all-gather.13.cloned.1.call-update) | async-done | bytes 23068688 | tf_op jit(solution)/shard_map/all_gather | solution.py:136
  911.2 18.7 multiply_convert_fusion.1
  929.9 22.1 multiply_reduce_fusion.4
  961.1 12.9 convolution_convert_fusion.1
  977.4 8.4 multiply_reduce_fusion.5
  1002.1 14.2 all-to-all-done.5
  1025.9 241.0 %while.44 = (s32[]{:T(128)}, f32[1,4,128,128]{2,3,1,0:T(8,128)S(1)}, f32[16,1,4,64,128]{4,3,2,1,0:T(8,128)}, f32[16,1,4,64,128]{4,3,2,1,0:T(8,128)}, f32[16,1,4,...) while((s32[]{:T(128)}, ...), condition=%wide.region_9.10_spmd.clone, body=%wide.region_8.9_spmd.clone.sunk | while | flops 352747520 | bytes 4728510 | solution.py:82
  1299.5 8.7 all-to-all-done.7
  1361.8 10.6 multiply_reduce_fusion.3
  1378.7 6.5 pad_add_fusion
  1393.8 14.0 convolution_convert_fusion.2
  1409.4 21.2 convolution_convert_fusion
  1436.1 8.7 all_to_all.105
  1450.2 204.2 %reduce-scatter.7.cloned.1.call-done = bf16[256,6144]{1,0:T(8,128)(2,1)} async-done(((bf16[2048,6144]{1,0:T(8,128)(2,1)}), bf16[256,6144]{1,0:T(8,128)(2,1)}) %reduce-scatter.7.cloned.1.call-update) | async-done | bytes 3145744 | tf_op jit(solution)/shard_map/reduce_scatter | solution.py:98
  1654.4 444.5 %reduce-scatter.13.cloned.1.call-done = bf16[256,11264]{1,0:T(8,128)(2,1)} async-done(((bf16[2048,11264]{1,0:T(8,128)(2,1)}), bf16[256,11264]{1,0:T(8,128)(2,1)}) %reduce-scatter.13.cloned.1.call-update) | async-done | bytes 5767184
  2099.6 12.6 fusion.105
  2114.0 14.4 fusion.110
  2128.4 38.2 %all-reduce.14 = (f32[2048]{0:T(1024)S(1)}, f32[128]{0:T(128)}, f32[2048]{0:T(1024)S(1)}) all-reduce(f32[2048]{0:T(1024)S(1)} %get-tuple-element.617, f32[128]{0:T(128)S(1)} %bitcast_reduce_fusion, f32[2048]{0:T(1024)S(1)} %copy-done.78), channel_id=1, replica_groups=mesh['fsdp'=8,'seq'=4] {'fsdp','seq'}, use_global_device_ids=true, to_apply=%region_16.17 | all-reduce | flops 4224 | bytes 33792 | tf_op jit(solution)/shard_map/psum | solution.py:242
  2171.4 58.3 %all-reduce.20.cloned.1.call-done = (f32[2048,16]{0,1:T(8,128)}, f32[2048,12]{0,1:T(8,128)}) async-done(((f32[2048,16]{0,1:T(8,128)}, f32[2048,12]{0,1:T(8,128)}), (f32[2048,16]{0,1:T(8,128)}, f32[2048,12]{0,1:T(8,128)})) %all-reduce.20.cloned.1.call-update) | async-done | bytes 229392 | tf_op jit(solution)/shard_map/psum | solution.py:242
  2232.4 246.7 %all-reduce.22.cloned.1.call-done = (bf16[256,6144]{1,0:T(8,128)(2,1)}, bf16[256,2048]{1,0:T(8,128)(2,1)}, bf16[256,11264]{1,0:T(8,128)(2,1)}, bf16[704,2048]{1,0:T(8,128)(2,1)}) async-done(((bf16[256,6144]{1,0:T(8,128)(2,1)}, bf16[256,2048]{1,0:T(8,128)(2,1)}, bf16[256,11264]{1,0:T(8,128)(2,1)}, bf16[704,2048]{1,0:T(8,128)(2,1)}), (bf16[256,6144]{1,0:T(8,128)(2,1)}, bf16[256,2048]{1,0:T(8,128)(2,1)}, ...) | async-done | bytes 12845072 | tf_op jit(solution)/shard_map/psum | solution.py:104
  (572 shorter events, 625.9 us)
Async XLA Ops:
  7.2 226.0 %all-gather.7.cloned.1.call-start = ((), (), s32[]{:S(2)}) async-start(), calls=%async_computation.14 | async-start | bytes 28311552 | tf_op jit(solution)/shard_map/all_gather | solution.py:128
  7.9 788.6 %all-gather.9.cloned.1.call-start = ((), (), s32[]{:S(2)}) async-start(), calls=%async_computation.15 | async-start | bytes 9437184 | tf_op jit(solution)/shard_map/all_gather | solution.py:131
  8.7 794.4 %all-gather.11.cloned.1.call-start = ((), (), s32[]{:S(2)}) async-start(), calls=%async_computation.16 | async-start | bytes 51904512 | tf_op jit(solution)/shard_map/all_gather | solution.py:133
  9.4 38.4 %copy-start.27 = (bf16[1,256,2048]{2,1,0:T(8,128)(2,1)S(1)}, bf16[1,256,2048]{2,1,0:T(8,128)(2,1)}, u32[]{:S(2)}) copy-start(bf16[1,256,2048]{2,1,0:T(8,128)(2,1)} %param.17) | copy-start | bytes 3145732
  9.4 901.7 %all-gather.13.cloned.1.call-start = ((), (), s32[]{:S(2)}) async-start(), calls=%async_computation.17 | async-start | bytes 25952256 | tf_op jit(solution)/shard_map/all_gather | solution.py:136
  10.1 44.6 %copy-start.77 = (bf16[256,12]{0,1:T(8,128)(2,1)S(1)}, bf16[256,12]{0,1:T(8,128)(2,1)}, u32[]{:S(2)}) copy-start(bf16[256,12]{0,1:T(8,128)(2,1)} %param.22) | copy-start | bytes 18436
  23.7 221.9 %copy-start.46 = (f32[8,1,256]{2,1,0:T(1,128)}, f32[8,1,256]{2,1,0:T(1,128)S(1)}, u32[]{:S(2)}) copy-start(f32[8,1,256]{2,1,0:T(1,128)S(1)} %convert_element_type.540) | copy-start | bytes 24580
  48.7 196.9 %copy-start.70 = (f32[256]{0:T(256)}, f32[256]{0:T(256)S(1)}, u32[]{:S(2)}) copy-start(f32[256]{0:T(256)S(1)} %fusion.204) | copy-start | bytes 3076
  51.0 211.7 %all-to-all-start.1 = ((bf16[4,2,512]{2,1,0:T(2,128)(2,1)}), bf16[4,2,512]{2,1,0:T(2,128)(2,1)S(1)}, u32[]{:S(2)}, u32[]{:S(2)}) async-start(bf16[4,2,512]{2,1,0:T(2,128)(2,1)} %reshape.1133), calls=%async_computation.1 | async-start | bytes 16384 | tf_op jit(solution)/shard_map/all_to_all | solution.py:161
  245.6 5.0 collective-permute-start
  262.7 18.6 all-to-all-start
  281.3 17.5 all-to-all-start.3
  299.8 17.3 all-to-all-start.2
  303.8 333.9 %copy-start.44 = (f32[64,64]{1,0:T(8,128)}, f32[64,64]{1,0:T(8,128)S(1)}, u32[]{:S(2)}) copy-start(f32[64,64]{1,0:T(8,128)S(1)} %fusion.200) | copy-start | bytes 49156
  764.0 17.3 all-to-all-start.4
  768.3 681.9 %reduce-scatter.9.cloned.1.call-start = ((), (), s32[]{:S(2)}) async-start(), calls=%async_computation.19 | async-start | bytes 9437184 | tf_op jit(solution)/shard_map/reduce_scatter | solution.py:98
  803.0 126.9 %copy-start.30 = (f32[256,2048]{1,0:T(8,128)}, f32[256,2048]{1,0:T(8,128)S(1)}, u32[]{:S(2)}) copy-start(f32[256,2048]{1,0:T(8,128)S(1)} %get-tuple-element.707) | copy-start | bytes 6291460
  955.2 22.1 copy-start.3
  961.1 489.1 %reduce-scatter.11.cloned.1.call-start = ((), (), s32[]{:S(2)}) async-start(), calls=%async_computation.20 | async-start | bytes 25952256 | tf_op jit(solution)/shard_map/reduce_scatter | solution.py:98
  998.0 18.3 all-to-all-start.5
  1025.9 241.0 %copy-start.8 = (f32[16,1,4,1,64,64]{4,5,3,2,1,0:T(8,128)S(1)}, f32[16,1,4,1,64,64]{4,5,3,2,1,0:T(8,128)}, u32[]{:S(2)}) copy-start(f32[16,1,4,1,64,64]{4,5,3,2,1,0:T(8,128)} %copy-done.7) | copy-start | bytes 3145732
  1290.5 17.7 all-to-all-start.7
  1308.2 20.7 all-to-all-start.8
  1328.9 21.0 all-to-all-start.6
  1333.2 321.2 %reduce-scatter.7.cloned.1.call-start = ((), (), s32[]{:S(2)}) async-start(), calls=%async_computation.18 | async-start | bytes 28311552 | tf_op jit(solution)/shard_map/reduce_scatter | solution.py:98
  1386.2 6.0 collective-permute-start.1
  1407.9 691.0 %reduce-scatter.13.cloned.1.call-start = ((), (), s32[]{:S(2)}) async-start(), calls=%async_computation.21 | async-start | bytes 51904512
  1430.7 16.8 copy-start.28
  1430.7 799.0 %all-reduce.20.cloned.1.call-start = ((), (), s32[]{:S(2)}) async-start(), calls=%async_computation.22 | async-start | bytes 524288 | tf_op jit(solution)/shard_map/psum | solution.py:242
  1450.1 1028.9 %all-reduce.22.cloned.1.call-start = ((), (), s32[]{:S(2)}) async-start(), calls=%async_computation.23 | async-start | bytes 25690112 | tf_op jit(solution)/shard_map/psum | solution.py:104
  2114.0 53.9 %copy-start.75 = (f32[256]{0:T(256)S(1)}, f32[256]{0:T(256)}, u32[]{:S(2)}) copy-start(f32[256]{0:T(256)} %copy-done.74) | copy-start | bytes 3076
  2114.0 54.0 %copy-start.4 = (f32[256,2048]{1,0:T(8,128)S(1)}, f32[256,2048]{1,0:T(8,128)}, u32[]{:S(2)}) copy-start(f32[256,2048]{1,0:T(8,128)} %copy-done.3) | copy-start | bytes 6291460
  (75 other events, 433.6 us)
Sparse Core Ops, SparseCore 0:
  9.7 223.4 all-gather.6
  234.8 80.2 all-gather.8
  316.8 391.8 all-gather.10
  710.1 200.9 all-gather.12
  961.2 87.8 reduce-scatter.8
  1051.2 225.7 reduce-scatter.10
  1408.0 246.3 reduce-scatter.6
  1656.8 442.0 reduce-scatter.12
  2106.1 123.5 all-reduce.19
  2234.0 244.9 all-reduce.21
where the time goes:
time: 2520 us; the launch traced here: 2500 us
  waiting for transfers between devices  1260 us (50%)
  matrix products  546 us (22%)
  other arithmetic  419 us (17%)
  blocking collectives  119 us (5%)
  local copies, waits for them, and re-layouts  103 us (4%)
  starting transfers between devices  41.7 us (2%)
    unnamed x11, waiting for transfers between devices  447 us
    another operation x5, other arithmetic, delta_rule(): lax.linalg.triangular_solve(system, targets, left_side=True, lower=True,...  318 us
    psum x1, waiting for transfers between devices, reduce_rows(): return lax.psum(summed, 'seq').astype(jnp.float32)  247 us
    reduce_scatter x3, waiting for transfers between devices, reduce_rows(): lax.psum_scatter(term(jnp.int32(0), total_rows // shards * lax.axis_size(...  204 us
    all_gather x1, waiting for transfers between devices, per_device(): lax.all_gather(w_qkv, 'fsdp', axis=0, tiled=True)  153 us
    dot_general x48, matrix products, advance(): result = jnp.einsum('shcd,shde->shce', query_part, state, precision=HIGH)  92.6 us
    dot_general x48, matrix products, advance(): jnp.einsum('shcd,shce->shde', key_raw, fresh, precision=HIGH)  90 us
    all_gather x1, waiting for transfers between devices, per_device(): down_full = lax.all_gather(w_down, 'fsdp', axis=0, tiled=True)  83.8 us
  transfers between devices with their start and end apart: 21, of which 14 were waited for; matrix products, arithmetic and copies ran while one was open for 39% of the time, Pallas kernels for 0%

commit v1 on v0

--- a/solution.py
+++ b/solution.py
@@ -239,10 +239,10 @@
     grad_residual_norm, grad_gain_first = first_back(grad_normed_first)
     grad_input = (grad_middle + grad_residual_norm).reshape(sequences, block, width)
     grad_conv = grad_table.reshape(3, width, -1).transpose(1, 0, 2).reshape(width, -1)
-    summed = lax.psum(
-        (grad_gain_first, grad_beta_full, grad_conv, grad_gain_heads, grad_gain_second),
-        ("fsdp", "seq"),
-    )
+    current_block = lax.psum(
+        (grad_gain_first, grad_beta_full, grad_conv, grad_gain_heads, grad_gain_second), "seq"
+    )
+    summed = lax.psum(current_block, "fsdp")
     share = width // lax.axis_size("fsdp")
     offset = lax.axis_index("fsdp") * share
 

time: 2520 us -> 2760 us (1.095)
  waiting for transfers between devices: 1260 us -> 1490 us
    reduce_scatter x3, waiting for transfers between devices: 204 us -> 529 us  [reduce_rows(): lax.psum_scatter(term(jnp.int32(0), total_rows // shards * lax.axis_size(...]
    psum x1, waiting for transfers between devices: 58.3 us -> 0.02 us  [per_device(): lax.psum((grad_gain_first, grad_beta_full, grad_conv, grad_gain_heads, gr...]
    unnamed x11 -> x12, waiting for transfers between devices: 447 us -> 448 us
  transfers between devices with their start and end apart: 21 -> 23, of which waited for: 14 -> 16; matrix products, arithmetic and copies ran while one was open for 39% -> 25% of each run, Pallas kernels for 0% -> 0%
where the time goes in v1:
time: 2760 us; the launch traced here: 2750 us
  waiting for transfers between devices  1490 us (54%)
  matrix products  563 us (20%)
  other arithmetic  415 us (15%)
  blocking collectives  115 us (4%)
  local copies, waits for them, and re-layouts  101 us (4%)
  starting transfers between devices  44.8 us (2%)
    reduce_scatter x3, waiting for transfers between devices, reduce_rows(): lax.psum_scatter(term(jnp.int32(0), total_rows // shards * lax.axis_size(...  529 us
    unnamed x12, waiting for transfers between devices  448 us
    another operation x5, other arithmetic, delta_rule(): lax.linalg.triangular_solve(system, targets, left_side=True, lower=True,...  318 us
    psum x1, waiting for transfers between devices, reduce_rows(): return lax.psum(summed, 'seq').astype(jnp.float32)  225 us
    all_gather x1, waiting for transfers between devices, per_device(): lax.all_gather(w_qkv, 'fsdp', axis=0, tiled=True)  153 us
    dot_general x48, matrix products, advance(): result = jnp.einsum('shcd,shde->shce', query_part, state, precision=HIGH)  92.2 us
    dot_general x48, matrix products, advance(): jnp.einsum('shcd,shde->shce', key_part, state, precision=HIGH)  91.3 us
    dot_general x48, matrix products, advance(): jnp.einsum('shcd,shce->shde', key_raw, fresh, precision=HIGH)  89.7 us
  transfers between devices with their start and end apart: 23, of which 16 were waited for; matrix products, arithmetic and copies ran while one was open for 25% of the time, Pallas kernels for 0%

profile of v1, /device:TPU:0, one launch (start us, length us, event | category | flops | bytes accessed | tf_op | source)
XLA Modules:
  0.0 2745.0 jit_solution(9402675148322685214)
XLA Ops:
  10.1 13.6 all-gather
  23.7 24.1 all_gather.27
  54.6 25.3 all_gather.26
  80.0 153.2 %all-gather.7.cloned.1.call-done = bf16[2048,6144]{1,0:T(8,128)(2,1)} async-done(((bf16[256,6144]{1,0:T(8,128)(2,1)}), bf16[2048,6144]{1,0:T(8,128)(2,1)}) %all-gather.7.cloned.1.call-update) | async-done | bytes 25165840 | tf_op jit(solution)/shard_map/all_gather | solution.py:128
  233.2 12.3 fusion.79
  268.2 12.8 all-to-all-done
  287.3 11.2 all-to-all-done.3
  307.0 9.6 all-to-all-done.2
  321.9 315.2 %custom-call.7 = f32[16,1,4,1,64,64]{4,5,3,2,1,0:T(8,128)S(1)} custom-call(f32[16,1,4,1,64,64]{5,4,3,2,1,0:T(8,128)} %add_bitcast_fusion), custom_call_target="InvertDiagBlocksLowerTriangular" | custom-call | tf_op jit(solution)/shard_map/jvp()/triangular_solve | solution.py:66
  652.9 117.3 %while.43 = (s32[]{:T(128)}, f32[1,4,128,128]{3,2,1,0:T(8,128)S(1)}, bf16[16,1,4,64,128]{4,3,0,2,1:T(8,128)(2,1)}, f32[16,1,4,128,128]{4,3,2,1,0:T(8,128)}, f32[...) while((s32[]{:T(128)}, ...), condition=%wide.region_3.4_spmd.clone, body=%wide.region_2.3_spmd.clone.sunk | while | flops 176553984 | bytes 3148948 | solution.py:82
  777.6 9.3 all-gather.1
  814.5 24.8 fusion.211
  839.3 71.8 %all-gather.13.cloned.1.call-done = bf16[5632,2048]{1,0:T(8,128)(2,1)} async-done(((bf16[704,2048]{1,0:T(8,128)(2,1)}), bf16[5632,2048]{1,0:T(8,128)(2,1)}) %all-gather.13.cloned.1.call-update) | async-done | bytes 23068688 | tf_op jit(solution)/shard_map/all_gather | solution.py:136
  911.2 18.7 multiply_convert_fusion.1
  929.9 22.4 multiply_reduce_fusion.4
  956.1 9.0 multiply_reduce_fusion.5
  981.3 14.4 all-to-all-done.5
  1006.7 240.2 %while.44 = (s32[]{:T(128)}, f32[1,4,128,128]{2,3,1,0:T(8,128)S(1)}, f32[16,1,4,64,128]{4,3,2,1,0:T(8,128)}, f32[16,1,4,64,128]{4,3,2,1,0:T(8,128)}, f32[16,1,4,...) while((s32[]{:T(128)}, ...), condition=%wide.region_9.10_spmd.clone, body=%wide.region_8.9_spmd.clone.sunk | while | flops 352747520 | bytes 4728510 | solution.py:82
  1246.9 8.2 fusion.86
  1350.9 10.0 multiply_reduce_fusion.3
  1371.7 12.1 convolution_convert_fusion.1
  1405.8 14.4 convolution_convert_fusion.2
  1421.8 21.3 convolution_convert_fusion
  1443.8 52.3 %reduce-scatter.9.cloned.1.call-done = bf16[256,2048]{1,0:T(8,128)(2,1)} async-done(((bf16[2048,2048]{1,0:T(8,128)(2,1)}), bf16[256,2048]{1,0:T(8,128)(2,1)}) %reduce-scatter.9.cloned.1.call-update) | async-done | bytes 1048592 | tf_op jit(solution)/shard_map/reduce_scatter | solution.py:98
  1496.1 228.3 %reduce-scatter.11.cloned.1.call-done = bf16[704,2048]{1,0:T(8,128)(2,1)} async-done(((bf16[5632,2048]{1,0:T(8,128)(2,1)}), bf16[704,2048]{1,0:T(8,128)(2,1)}) %reduce-scatter.11.cloned.1.call-update) | async-done | bytes 2883600 | tf_op jit(solution)/shard_map/reduce_scatter | solution.py:98
  1724.4 248.0 %reduce-scatter.7.cloned.1.call-done = bf16[256,6144]{1,0:T(8,128)(2,1)} async-done(((bf16[2048,6144]{1,0:T(8,128)(2,1)}), bf16[256,6144]{1,0:T(8,128)(2,1)}) %reduce-scatter.7.cloned.1.call-update) | async-done | bytes 3145744 | tf_op jit(solution)/shard_map/reduce_scatter | solution.py:98
  1972.4 444.6 %reduce-scatter.13.cloned.1.call-done = bf16[256,11264]{1,0:T(8,128)(2,1)} async-done(((bf16[2048,11264]{1,0:T(8,128)(2,1)}), bf16[256,11264]{1,0:T(8,128)(2,1)}) %reduce-scatter.13.cloned.1.call-update) | async-done | bytes 5767184
  2417.8 12.4 fusion.105
  2431.9 14.5 fusion.110
  2446.4 16.1 all-reduce.16
  2462.5 26.7 all-reduce.14
  2496.7 225.4 %all-reduce.27.cloned.1.call-done = (bf16[256,6144]{1,0:T(8,128)(2,1)}, bf16[256,2048]{1,0:T(8,128)(2,1)}, bf16[256,11264]{1,0:T(8,128)(2,1)}, bf16[704,2048]{1,0:T(8,128)(2,1)}) async-done(((bf16[256,6144]{1,0:T(8,128)(2,1)}, bf16[256,2048]{1,0:T(8,128)(2,1)}, bf16[256,11264]{1,0:T(8,128)(2,1)}, bf16[704,2048]{1,0:T(8,128)(2,1)}), (bf16[256,6144]{1,0:T(8,128)(2,1)}, bf16[256,2048]{1,0:T(8,128)(2,1)}, ...) | async-done | bytes 12845072 | tf_op jit(solution)/shard_map/psum | solution.py:104
  (549 shorter events, 646.3 us)
Async XLA Ops:
  7.2 226.0 %all-gather.7.cloned.1.call-start = ((), (), s32[]{:S(2)}) async-start(), calls=%async_computation.14 | async-start | bytes 28311552 | tf_op jit(solution)/shard_map/all_gather | solution.py:128
  7.9 798.8 %all-gather.9.cloned.1.call-start = ((), (), s32[]{:S(2)}) async-start(), calls=%async_computation.15 | async-start | bytes 9437184 | tf_op jit(solution)/shard_map/all_gather | solution.py:131
  8.7 805.8 %all-gather.11.cloned.1.call-start = ((), (), s32[]{:S(2)}) async-start(), calls=%async_computation.16 | async-start | bytes 51904512 | tf_op jit(solution)/shard_map/all_gather | solution.py:133
  9.4 14.2 copy-start.62
  9.4 38.4 %copy-start.24 = (bf16[1,256,2048]{2,1,0:T(8,128)(2,1)S(1)}, bf16[1,256,2048]{2,1,0:T(8,128)(2,1)}, u32[]{:S(2)}) copy-start(bf16[1,256,2048]{2,1,0:T(8,128)(2,1)} %param.17) | copy-start | bytes 3145732
  9.4 901.7 %all-gather.13.cloned.1.call-start = ((), (), s32[]{:S(2)}) async-start(), calls=%async_computation.17 | async-start | bytes 25952256 | tf_op jit(solution)/shard_map/all_gather | solution.py:136
  10.1 44.6 %copy-start.63 = (bf16[256,12]{0,1:T(8,128)(2,1)S(1)}, bf16[256,12]{0,1:T(8,128)(2,1)}, u32[]{:S(2)}) copy-start(bf16[256,12]{0,1:T(8,128)(2,1)} %param.22) | copy-start | bytes 18436
  23.7 221.9 %copy-start.39 = (f32[8,1,256]{2,1,0:T(1,128)}, f32[8,1,256]{2,1,0:T(1,128)S(1)}, u32[]{:S(2)}) copy-start(f32[8,1,256]{2,1,0:T(1,128)S(1)} %convert_element_type.540) | copy-start | bytes 24580
  48.7 196.9 %copy-start.57 = (f32[256]{0:T(256)}, f32[256]{0:T(256)S(1)}, u32[]{:S(2)}) copy-start(f32[256]{0:T(256)S(1)} %fusion.204) | copy-start | bytes 3076
  51.0 211.4 %all-to-all-start.1 = ((bf16[4,2,512]{2,1,0:T(2,128)(2,1)}), bf16[4,2,512]{2,1,0:T(2,128)(2,1)S(1)}, u32[]{:S(2)}, u32[]{:S(2)}) async-start(bf16[4,2,512]{2,1,0:T(2,128)(2,1)} %reshape.1133), calls=%async_computation.1 | async-start | bytes 16384 | tf_op jit(solution)/shard_map/all_to_all | solution.py:161
  245.6 4.9 collective-permute-start
  262.4 18.6 all-to-all-start
  281.0 17.6 all-to-all-start.3
  299.5 17.0 all-to-all-start.2
  773.4 17.4 all-to-all-start.4
  977.0 18.6 all-to-all-start.5
  1270.1 15.0 all-to-all-start.9
  1285.1 17.8 all-to-all-start.7
  1302.9 16.8 all-to-all-start.8
  1319.7 19.3 all-to-all-start.6
  1324.0 119.3 %all-reduce.25.cloned.1.call-start = ((), (), s32[]{:S(2)}) async-start(), calls=%async_computation.23 | async-start | bytes 524288 | tf_op jit(solution)/shard_map/psum | solution.py:242
  1361.7 134.4 %reduce-scatter.9.cloned.1.call-start = ((), (), s32[]{:S(2)}) async-start(), calls=%async_computation.19 | async-start | bytes 9437184 | tf_op jit(solution)/shard_map/reduce_scatter | solution.py:98
  1369.9 354.5 %reduce-scatter.11.cloned.1.call-start = ((), (), s32[]{:S(2)}) async-start(), calls=%async_computation.20 | async-start | bytes 25952256 | tf_op jit(solution)/shard_map/reduce_scatter | solution.py:98
  1383.9 588.6 %reduce-scatter.7.cloned.1.call-start = ((), (), s32[]{:S(2)}) async-start(), calls=%async_computation.18 | async-start | bytes 28311552 | tf_op jit(solution)/shard_map/reduce_scatter | solution.py:98
  1398.4 6.0 collective-permute-start.1
  1405.8 14.4 copy-start.23
  1420.3 996.8 %reduce-scatter.13.cloned.1.call-start = ((), (), s32[]{:S(2)}) async-start(), calls=%async_computation.21 | async-start | bytes 51904512
  1443.2 1050.8 %all-reduce.23.cloned.1.call-start = ((), (), s32[]{:S(2)}) async-start(), calls=%async_computation.22 | async-start | bytes 524288 | tf_op jit(solution)/shard_map/psum | solution.py:245
  1443.8 1278.3 %all-reduce.27.cloned.1.call-start = ((), (), s32[]{:S(2)}) async-start(), calls=%async_computation.24 | async-start | bytes 25690112 | tf_op jit(solution)/shard_map/psum | solution.py:104
  2431.9 14.5 copy-start.64
  2431.9 58.6 %copy-start.61 = (f32[256]{0:T(256)S(1)}, f32[256]{0:T(256)}, u32[]{:S(2)}) copy-start(f32[256]{0:T(256)} %copy-done.60) | copy-start | bytes 3076
  2431.9 58.6 %copy-start.3 = (f32[256,2048]{1,0:T(8,128)S(1)}, f32[256,2048]{1,0:T(8,128)}, u32[]{:S(2)}) copy-start(f32[256,2048]{1,0:T(8,128)} %copy-done.2) | copy-start | bytes 6291460
  (63 other events, 247.8 us)
Sparse Core Ops, SparseCore 0:
  9.7 223.4 all-gather.6
  234.8 80.2 all-gather.8
  316.8 391.8 all-gather.10
  710.1 201.0 all-gather.12
  1361.8 41.7 all-reduce.24
  1406.4 89.6 reduce-scatter.8
  1498.6 225.7 reduce-scatter.10
  1726.9 245.5 reduce-scatter.6
  1974.9 442.0 reduce-scatter.12
  2419.2 53.4 all-reduce.22
  2477.2 244.8 all-reduce.26
